TPU v7x, 32 devices: a whole 2x2x4 slice. The times are simulated.
32 devices in a mesh: rows: 8 (over y, x, core), feat: 4 (over z).
Axes of the slice: x: 2, y: 2, z: 4, core: 2. Of those that a mesh axis runs over, the one named last changes fastest.
Arguments:
- features: bfloat16 [1536, 16384], P('rows', 'feat'), may hold values from -0.5 to 0.5
- labels: int32 [1536], P('rows'), may hold values 0 or 1
- posterior: bfloat16 [16384], P('feat'), may hold values from -1 to 1
- prior_prec: float32 [16384], P('feat'), may hold values from 1 to 10
Outputs:
- hessian: float32 [16384, 16384], P('feat', 'rows')
- gradient: float32 [16384], P('feat')
All inputs are finite; a program needn't handle non-finite values. No bound on the sum of `labels` on one device may be relied on, other than what follows from the above.
Results may differ from a plain program's by a relative error of at most 0.003.
Values may be sent and summed in bfloat16 or wider, within the bound.
A program may use at most 128 MiB of HBM per device.

v0:
```python
import jax
import jax.numpy as jnp
from jax import lax
from jax.sharding import PartitionSpec as P


def per_device(features, labels, posterior, prior_prec):
    row_count = lax.axis_size("rows")
    feat_count = lax.axis_size("feat")
    row_index = lax.axis_index("rows")
    feat_index = lax.axis_index("feat")
    block_width = features.shape[1]
    col_width = block_width * feat_count // row_count
    partial_value = jnp.dot(features, posterior, preferred_element_type=jnp.float32)
    margins = lax.psum(partial_value, "feat")
    chance = jax.nn.sigmoid(margins)
    weight = (chance * (1.0 - chance)).astype(jnp.bfloat16)
    residual = (labels.astype(jnp.float32) - chance).astype(jnp.bfloat16)
    all_rows, all_weight = (
        lax.all_gather(features, "rows", axis=0, tiled=True),
        lax.all_gather(weight, "rows", axis=0, tiled=True),
    )
    local_grad = jnp.dot(residual, features, preferred_element_type=jnp.float32)
    summed = lax.psum(local_grad, "rows")
    gradient = summed - prior_prec * posterior.astype(jnp.float32)
    full_width = lax.all_gather(features, "feat", axis=1, tiled=True)
    column_rows = lax.all_to_all(full_width, "rows", split_axis=1, concat_axis=0, tiled=True)
    weighted = all_weight[:, None] * all_rows
    product = lax.dot_general(
        weighted, column_rows, (((0,), (0,)), ((), ())), preferred_element_type=jnp.float32
    )
    global_rows = feat_index * block_width + jnp.arange(block_width, dtype=jnp.int32)
    global_cols = row_index * col_width + jnp.arange(col_width, dtype=jnp.int32)
    on_diagonal = global_rows[:, None] == global_cols[None, :]
    hessian = product + jnp.where(on_diagonal, prior_prec[:, None], jnp.float32(0.0))
    return (hessian, gradient)


def solution(mesh):
    in_specs = (P("rows", "feat"), P("rows"), P("feat"), P("feat"))
    out_specs = (P("feat", "rows"), P("feat"))
    return jax.shard_map(
        per_device, mesh=mesh, in_specs=in_specs, out_specs=out_specs, check_vma=False
    )
```

profile of v0, /device:TPU:0, one launch (start us, length us, event | category | flops | bytes accessed | tf_op | source)
XLA Modules:
  0.0 306.3 jit_solution(11984968131884465313)
XLA Ops:
  7.2 0.0 all-gather.5.cloned.1.call-start
  7.2 0.7 all-gather.5.cloned.1.call-update
  7.9 0.0 all-gather.3.cloned.1.call-start
  7.9 0.7 all-gather.3.cloned.1.call-update
  8.6 119.0 %all-gather.5.cloned.1.call-done = bf16[192,16384]{1,0:T(8,128)(2,1)} async-done(((bf16[192,4096]{1,0:T(8,128)(2,1)}), bf16[192,16384]{1,0:T(8,128)(2,1)}) %all-gather.5.cloned.1.call-update) | async-done | bytes 6291472 | tf_op jit(solution)/shard_map/all_gather | solution.py:26
  127.6 0.0 copy-start.1
  127.6 0.0 copy-start
  127.6 0.0 copy-start.3
  127.6 0.0 copy-start.4
  127.6 0.0 copy-start.2
  127.6 6.7 %copy.10 = bf16[24,8,8,2048]{3,2,0,1:T(8,128)(2,1)} copy(bf16[24,8,8,2048]{3,2,1,0:T(8,128)(2,1)} %bitcast.16) | data formatting | bytes 12582912 | tf_op jit(solution)/shard_map/all_to_all | solution.py:27
  134.4 4.9 %all-to-all-start = ((bf16[192,8,2048]{2,0,1:T(8,128)(2,1)}), bf16[192,8,2048]{2,0,1:T(8,128)(2,1)}, u32[]{:S(2)}, u32[]{:S(2)}) async-start(bf16[192,8,2048]{2,0,1:T(8,128)(2,1)} %bitcast.15), calls=%async_computation | async-start | bytes 12582912 | tf_op jit(solution)/shard_map/all_to_all | solution.py:27
  139.3 0.0 copy-done.1
  139.3 0.0 copy-done
  139.3 0.5 fusion.3
  139.8 8.6 %psum.14 = f32[192]{0:T(256)S(1)} all-reduce(f32[192]{0:T(256)S(1)} %bitcast.18), channel_id=1, replica_groups=mesh['rows'=8,'feat'=4] {'feat'}, use_global_device_ids=true, to_apply=%region_0.0 | all-reduce | flops 192 | bytes 1536 | tf_op jit(solution)/shard_map/psum | solution.py:15
  148.4 0.0 copy-done.3
  148.4 0.0 copy-done.4
  148.4 0.6 dynamic-slice
  149.7 0.2 dynamic-update-slice
  149.9 90.2 %all-reduce = bf16[1536]{0:T(1024)(128)(2,1)S(1)} all-reduce(bf16[1536]{0:T(1024)(128)(2,1)S(1)} %dynamic-update-slice), channel_id=1, replica_groups=mesh['rows'=8,'feat'=4] {'rows'}, use_global_device_ids=true, to_apply=%add | all-reduce | flops 1536 | bytes 6144
  240.1 0.3 fusion.4
  240.4 23.5 %psum.15 = f32[4096]{0:T(1024)S(1)} all-reduce(f32[4096]{0:T(1024)S(1)} %bitcast.17), channel_id=1, replica_groups=mesh['rows'=8,'feat'=4] {'rows'}, use_global_device_ids=true, to_apply=%region_1.0 | all-reduce | flops 4096 | bytes 32768 | tf_op jit(solution)/shard_map/psum | solution.py:24
  263.9 0.0 copy-done.2
  264.0 0.6 multiply_subtract_fusion
  264.6 0.0 all-to-all-done
  264.6 0.0 all-gather.3.cloned.1.call-done
  264.6 34.9 %select_add_fusion = f32[4096,2048]{1,0:T(8,128)} fusion(bf16[1536,2048]{1,0:T(8,128)(2,1)} %bitcast.3, f32[4096]{0:T(1024)S(1)} %copy-done.2, s32[2048]{0:T(1024)S(1)} %iota_add_fusion.1, s32[4096]{0:T(1024)S(1)} %iota_add_fusion, bf16[1536,4096]{1,0:T(8,128)(2,1)} %all-gather.3.cloned.1.call-done, bf16[1536]{0:T(1024)(128)(2,1)S(1)} %all-reduce), kind=kOutput, calls=%fused_computation | convolution fusion | flops 25801261056 | bytes 52472832 | tf_op jit(solution)/shard_map/dot_general | solution.py:29
  (7 shorter events, 0.0 us)
Async XLA Ops:
  7.2 120.5 %all-gather.5.cloned.1.call-start = ((), (), s32[]{:S(2)}) async-start(), calls=%async_computation.2 | async-start | bytes 7864320 | tf_op jit(solution)/shard_map/all_gather | solution.py:26
  7.9 256.7 %all-gather.3.cloned.1.call-start = ((), (), s32[]{:S(2)}) async-start(), calls=%async_computation.1 | async-start | bytes 14155776 | tf_op jit(solution)/shard_map/all_gather | solution.py:20
  127.6 11.6 %copy-start.1 = (bf16[4096]{0:T(1024)(128)(2,1)S(1)}, bf16[4096]{0:T(1024)(128)(2,1)}, u32[]{:S(2)}) copy-start(bf16[4096]{0:T(1024)(128)(2,1)} %param.6) | copy-start | bytes 24580
  127.6 11.7 %copy-start = (bf16[192,4096]{1,0:T(8,128)(2,1)S(1)}, bf16[192,4096]{1,0:T(8,128)(2,1)}, u32[]{:S(2)}) copy-start(bf16[192,4096]{1,0:T(8,128)(2,1)} %param.4) | copy-start | bytes 4718596
  127.6 20.7 %copy-start.3 = (s32[192]{0:T(256)S(1)}, s32[192]{0:T(256)}, u32[]{:S(2)}) copy-start(s32[192]{0:T(256)} %param.5) | copy-start | bytes 2308
  127.6 20.8 %copy-start.4 = (u32[32]{0:T(128)S(1)}, u32[32]{0:T(128)}, u32[]{:S(2)}) copy-start(u32[32]{0:T(128)} %constant.19) | copy-start | bytes 388
  127.6 136.3 %copy-start.2 = (f32[4096]{0:T(1024)S(1)}, f32[4096]{0:T(1024)}, u32[]{:S(2)}) copy-start(f32[4096]{0:T(1024)} %param.7) | copy-start | bytes 49156
  134.4 130.2 %all-to-all-start = ((bf16[192,8,2048]{2,0,1:T(8,128)(2,1)}), bf16[192,8,2048]{2,0,1:T(8,128)(2,1)}, u32[]{:S(2)}, u32[]{:S(2)}) async-start(bf16[192,8,2048]{2,0,1:T(8,128)(2,1)} %bitcast.15), calls=%async_computation | async-start | bytes 12582912 | tf_op jit(solution)/shard_map/all_to_all | solution.py:27
Sparse Core Ops, SparseCore 0:
  9.5 118.0 all-gather.4
  129.5 130.8 all-gather.2
where the time goes:
time: 307 us; the launch traced here: 306 us
  blocking collectives  122 us (40%)
  waiting for transfers between devices  120 us (39%)
  matrix products  35.7 us (12%)
  between operations  14.8 us (5%)
  local copies, waits for them, and re-layouts  7.61 us (2%)
  starting transfers between devices  4.94 us (2%)
    all_gather x1, waiting for transfers between devices, per_device(): full_width = lax.all_gather(features, 'feat', axis=1, tiled=True)  119 us
    unnamed x1, blocking collectives  90.2 us
    dot_general x1, matrix products, per_device(): lax.dot_general(weighted, column_rows, (((0,), (0,)), ((), ())), preferre...  34.9 us
    psum x1, blocking collectives, per_device(): summed = lax.psum(local_grad, 'rows')  23.5 us
    psum x1, blocking collectives, per_device(): margins = lax.psum(partial_value, 'feat')  8.57 us
    all_to_all x1, local copies, waits for them, and re-layouts, per_device(): lax.all_to_all(full_width, 'rows', split_axis=1, concat_axis=0, tiled=True)  6.73 us
  transfers between devices with their start and end apart: 3, of which 1 were waited for; matrix products, arithmetic and copies ran while one was open for 3% of the time, Pallas kernels for 0%

commit v1 on v0

--- a/solution.py
+++ b/solution.py
@@ -23,7 +23,12 @@
     local_grad = jnp.dot(residual, features, preferred_element_type=jnp.float32)
     summed = lax.psum(local_grad, "rows")
     gradient = summed - prior_prec * posterior.astype(jnp.float32)
-    full_width = lax.all_gather(features, "feat", axis=1, tiled=True)
+    ring = [features]
+    for hop in range(3):
+        ring.append(lax.ppermute(ring[-1], "feat", [(dev, (dev + 1) % 4) for dev in range(4)]))
+    full_width = jnp.roll(
+        jnp.concatenate(ring[::-1], axis=1), (lax.axis_index("feat") + 1) * ring[0].shape[1], axis=1
+    )
     column_rows = lax.all_to_all(full_width, "rows", split_axis=1, concat_axis=0, tiled=True)
     weighted = all_weight[:, None] * all_rows
     product = lax.dot_general(

time: 307 us -> 294 us (0.958)
  blocking collectives: 122 us -> 98.2 us
  local copies, waits for them, and re-layouts: 7.61 us -> 24.7 us
  waiting for transfers between devices: 120 us -> 112 us
    all_gather x1 -> x0, waiting for transfers between devices: 119 us -> none  [per_device(): full_width = lax.all_gather(features, 'feat', axis=1, tiled=True)]
    ppermute x0 -> x3, waiting for transfers between devices: none -> 111 us  [per_device(): lax.ppermute(ring[-1], 'feat', [(dev, (dev + 1) % 4) for dev in range(4)])]
    unnamed x1, blocking collectives: 90.2 us -> 67.5 us
    unnamed x14 -> x21, local copies, waits for them, and re-layouts: 0.87 us -> 16.9 us
    all_to_all x1, local copies, waits for them, and re-layouts: 6.73 us -> 3.28 us  [per_device(): lax.all_to_all(full_width, 'rows', split_axis=1, concat_axis=0, tiled=True)]
    dynamic_slice x0 -> x1, local copies, waits for them, and re-layouts: none -> 3.2 us  [per_device(): jnp.roll(jnp.concatenate(ring[::-1], axis=1), (lax.axis_index('feat') + 1...]
    ppermute x0 -> x3, starting transfers between devices: none -> 3.11 us  [per_device(): lax.ppermute(ring[-1], 'feat', [(dev, (dev + 1) % 4) for dev in range(4)])]
  transfers between devices with their start and end apart: 3 -> 5, of which waited for: 1 -> 3; matrix products, arithmetic and copies ran while one was open for 3% -> 9% of each run, Pallas kernels for 0% -> 0%
where the time goes in v1:
time: 294 us; the launch traced here: 293 us
  waiting for transfers between devices  112 us (38%)
  blocking collectives  98.2 us (33%)
  matrix products  35.6 us (12%)
  local copies, waits for them, and re-layouts  24.7 us (8%)
  between operations  14.8 us (5%)
  starting transfers between devices  7.95 us (3%)
    ppermute x3, waiting for transfers between devices, per_device(): lax.ppermute(ring[-1], 'feat', [(dev, (dev + 1) % 4) for dev in range(4)])  111 us
    unnamed x1, blocking collectives  67.5 us
    dot_general x1, matrix products, per_device(): lax.dot_general(weighted, column_rows, (((0,), (0,)), ((), ())), preferre...  34.8 us
    psum x1, blocking collectives, per_device(): summed = lax.psum(local_grad, 'rows')  22.3 us
    unnamed x21, local copies, waits for them, and re-layouts  16.9 us
    psum x1, blocking collectives, per_device(): margins = lax.psum(partial_value, 'feat')  8.35 us
  transfers between devices with their start and end apart: 5, of which 3 were waited for; matrix products, arithmetic and copies ran while one was open for 9% of the time, Pallas kernels for 0%

profile of v1, /device:TPU:0, one launch (start us, length us, event | category | flops | bytes accessed | tf_op | source)
XLA Modules:
  0.0 293.4 jit_solution(17414135304795943936)
XLA Ops:
  7.2 0.0 copy-start
  7.2 0.0 all-gather.2.cloned.1.call-start
  7.2 0.7 all-gather.2.cloned.1.call-update
  7.9 3.1 %collective-permute-start = (bf16[192,4096]{1,0:T(8,128)(2,1)}, bf16[192,4096]{1,0:T(8,128)(2,1)S(1)}, u32[]{:S(2)}, u32[]{:S(2)}) collective-permute-start(bf16[192,4096]{1,0:T(8,128)(2,1)} %param.4), channel_id=1, source_target_pairs={{0,1},{1,2},{2,3},{3,0},{4,5},{5,6},{6,7},{7,4},{8,9},{9,10},{10,1... | collective-permute-start | bytes 4718600 | tf_op jit(solution)/shard_map/ppermute | solution.py:28
  11.0 36.6 %collective-permute-done = bf16[192,4096]{1,0:T(8,128)(2,1)S(1)} collective-permute-done((bf16[192,4096]{1,0:T(8,128)(2,1)}, bf16[192,4096]{1,0:T(8,128)(2,1)S(1)}, u32[]{:S(2)}, u32[]{:S(2)}) %collective-permute-start) | collective-permute-done | bytes 1572896 | tf_op jit(solution)/shard_map/ppermute | solution.py:28
  47.6 0.0 collective-permute-start.1
  47.6 37.5 %collective-permute-done.1 = bf16[192,4096]{1,0:T(8,128)(2,1)} collective-permute-done((bf16[192,4096]{1,0:T(8,128)(2,1)S(1)}, bf16[192,4096]{1,0:T(8,128)(2,1)}, u32[]{:S(2)}, u32[]{:S(2)}) %collective-permute-start.1) | collective-permute-done | bytes 1572896 | tf_op jit(solution)/shard_map/ppermute | solution.py:28
  85.1 36.8 %collective-permute-done.2 = bf16[192,4096]{1,0:T(8,128)(2,1)} collective-permute-done((bf16[192,4096]{1,0:T(8,128)(2,1)}, bf16[192,4096]{1,0:T(8,128)(2,1)}, u32[]{:S(2)}, u32[]{:S(2)}) %collective-permute-start.2) | collective-permute-done | bytes 1572896 | tf_op jit(solution)/shard_map/ppermute | solution.py:28
  121.9 2.7 constant_dynamic-update-slice_fusion.7
  124.6 2.7 constant_dynamic-update-slice_fusion.6
  127.3 1.2 constant_dynamic-update-slice_fusion.5
  128.6 2.7 constant_dynamic-update-slice_fusion.4
  131.3 2.7 constant_dynamic-update-slice_fusion.3
  134.0 2.7 constant_dynamic-update-slice_fusion.2
  136.7 1.2 constant_dynamic-update-slice_fusion.1
  137.9 1.3 constant_dynamic-update-slice_fusion
  139.2 3.2 %constant_dynamic-slice_fusion = bf16[192,16384]{1,0:T(8,128)(2,1)S(1)} fusion(bf16[192,32768]{1,0:T(8,128)(2,1)} %constant_dynamic-update-slice_fusion, s32[]{:T(128)S(6)} %select_n.18), kind=kLoop, calls=%fused_computation.19 | loop fusion | bytes 12582916 | tf_op jit(solution)/shard_map/jit(_roll_dynamic)/dynamic_slice | solution.py:29
  142.4 0.0 copy-start.1
  142.5 0.0 copy-start.3
  142.5 0.0 copy-start.4
  142.5 0.0 copy-start.2
  142.5 3.3 %copy.10 = bf16[24,8,8,2048]{3,2,0,1:T(8,128)(2,1)} copy(bf16[24,8,8,2048]{3,2,1,0:T(8,128)(2,1)S(1)} %bitcast.16) | data formatting | bytes 12582912 | tf_op jit(solution)/shard_map/all_to_all | solution.py:32
  145.8 4.8 %all-to-all-start = ((bf16[192,8,2048]{2,0,1:T(8,128)(2,1)}), bf16[192,8,2048]{2,0,1:T(8,128)(2,1)}, u32[]{:S(2)}, u32[]{:S(2)}) async-start(bf16[192,8,2048]{2,0,1:T(8,128)(2,1)} %bitcast.15), calls=%async_computation | async-start | bytes 12582912 | tf_op jit(solution)/shard_map/all_to_all | solution.py:32
  150.6 0.5 fusion.3
  151.1 8.4 %psum.14 = f32[192]{0:T(256)S(1)} all-reduce(f32[192]{0:T(256)S(1)} %bitcast.18), channel_id=1, replica_groups=mesh['rows'=8,'feat'=4] {'feat'}, use_global_device_ids=true, to_apply=%region_0.0 | all-reduce | flops 192 | bytes 1536 | tf_op jit(solution)/shard_map/psum | solution.py:15
  159.5 0.6 dynamic-slice
  160.8 0.2 dynamic-update-slice
  161.0 67.5 %all-reduce = bf16[1536]{0:T(1024)(128)(2,1)S(1)} all-reduce(bf16[1536]{0:T(1024)(128)(2,1)S(1)} %dynamic-update-slice), channel_id=1, replica_groups=mesh['rows'=8,'feat'=4] {'rows'}, use_global_device_ids=true, to_apply=%add | all-reduce | flops 1536 | bytes 6144
  228.5 0.3 fusion.4
  228.8 22.3 %psum.15 = f32[4096]{0:T(1024)S(1)} all-reduce(f32[4096]{0:T(1024)S(1)} %bitcast.17), channel_id=1, replica_groups=mesh['rows'=8,'feat'=4] {'rows'}, use_global_device_ids=true, to_apply=%region_1.0 | all-reduce | flops 4096 | bytes 32768 | tf_op jit(solution)/shard_map/psum | solution.py:24
  251.2 0.6 multiply_subtract_fusion
  251.8 34.8 %select_add_fusion = f32[4096,2048]{1,0:T(8,128)} fusion(bf16[1536,2048]{1,0:T(8,128)(2,1)} %bitcast.3, f32[4096]{0:T(1024)S(1)} %copy-done.2, s32[2048]{0:T(1024)S(1)} %iota_add_fusion.1, s32[4096]{0:T(1024)S(1)} %iota_add_fusion, bf16[1536,4096]{1,0:T(8,128)(2,1)} %all-gather.2.cloned.1.call-done, bf16[1536]{0:T(1024)(128)(2,1)S(1)} %all-reduce), kind=kOutput, calls=%fused_computation | convolution fusion | flops 25801261056 | bytes 52472832 | tf_op jit(solution)/shard_map/dot_general | solution.py:34
  (15 shorter events, 0.1 us)
Async XLA Ops:
  7.2 130.8 %copy-start = (bf16[192,4096]{1,0:T(8,128)(2,1)S(1)}, bf16[192,4096]{1,0:T(8,128)(2,1)}, u32[]{:S(2)}) copy-start(bf16[192,4096]{1,0:T(8,128)(2,1)} %param.4) | copy-start | bytes 4718596
  7.2 244.6 %all-gather.2.cloned.1.call-start = ((), (), s32[]{:S(2)}) async-start(), calls=%async_computation.1 | async-start | bytes 14155776 | tf_op jit(solution)/shard_map/all_gather | solution.py:20
  7.9 39.7 %collective-permute-start = (bf16[192,4096]{1,0:T(8,128)(2,1)}, bf16[192,4096]{1,0:T(8,128)(2,1)S(1)}, u32[]{:S(2)}, u32[]{:S(2)}) collective-permute-start(bf16[192,4096]{1,0:T(8,128)(2,1)} %param.4), channel_id=1, source_target_pairs={{0,1},{1,2},{2,3},{3,0},{4,5},{5,6},{6,7},{7,4},{8,9},{9,10},{10,1... | collective-permute-start | bytes 4718600 | tf_op jit(solution)/shard_map/ppermute | solution.py:28
  47.6 37.5 %collective-permute-start.1 = (bf16[192,4096]{1,0:T(8,128)(2,1)S(1)}, bf16[192,4096]{1,0:T(8,128)(2,1)}, u32[]{:S(2)}, u32[]{:S(2)}) collective-permute-start(bf16[192,4096]{1,0:T(8,128)(2,1)S(1)} %collective-permute-done), channel_id=1, source_target_pairs={{0,1},{1,2},{2,3},{3,0},{4,5},{5,6},{6,7},{7,4},{8,9},{9,10},{10,1... | collective-permute-start | bytes 4718600 | tf_op jit(solution)/shard_map/ppermute | solution.py:28
  85.1 36.8 %collective-permute-start.2 = (bf16[192,4096]{1,0:T(8,128)(2,1)}, bf16[192,4096]{1,0:T(8,128)(2,1)}, u32[]{:S(2)}, u32[]{:S(2)}) collective-permute-start(bf16[192,4096]{1,0:T(8,128)(2,1)} %collective-permute-done.1), channel_id=1, source_target_pairs={{0,1},{1,2},{2,3},{3,0},{4,5},{5,6},{6,7},{7,4},{8,9},{9,10},{10,1... | collective-permute-start | bytes 4718600 | tf_op jit(solution)/shard_map/ppermute | solution.py:28
  142.4 8.1 %copy-start.1 = (bf16[4096]{0:T(1024)(128)(2,1)S(1)}, bf16[4096]{0:T(1024)(128)(2,1)}, u32[]{:S(2)}) copy-start(bf16[4096]{0:T(1024)(128)(2,1)} %param.6) | copy-start | bytes 24580
  142.5 17.0 %copy-start.3 = (s32[192]{0:T(256)S(1)}, s32[192]{0:T(256)}, u32[]{:S(2)}) copy-start(s32[192]{0:T(256)} %param.5) | copy-start | bytes 2308
  142.5 17.0 %copy-start.4 = (u32[32]{0:T(128)S(1)}, u32[32]{0:T(128)}, u32[]{:S(2)}) copy-start(u32[32]{0:T(128)} %constant.43) | copy-start | bytes 388
  142.5 108.7 %copy-start.2 = (f32[4096]{0:T(1024)S(1)}, f32[4096]{0:T(1024)}, u32[]{:S(2)}) copy-start(f32[4096]{0:T(1024)} %param.7) | copy-start | bytes 49156
  145.8 106.0 %all-to-all-start = ((bf16[192,8,2048]{2,0,1:T(8,128)(2,1)}), bf16[192,8,2048]{2,0,1:T(8,128)(2,1)}, u32[]{:S(2)}, u32[]{:S(2)}) async-start(bf16[192,8,2048]{2,0,1:T(8,128)(2,1)} %bitcast.15), calls=%async_computation | async-start | bytes 12582912 | tf_op jit(solution)/shard_map/all_to_all | solution.py:32
Sparse Core Ops, SparseCore 0:
  9.9 74.7 all-gather.1
